TPU v7x, 32 devices: a whole 2x2x4 slice. The times are simulated.
32 devices in a mesh: dp: 16 (over z, x, core), mp: 2 (over y).
Axes of the slice: x: 2, y: 2, z: 4, core: 2. Of those that a mesh axis runs over, the one named last changes fastest.
Arguments:
- tokens: bfloat16 [4, 384, 15, 1024], P(None, 'dp'), may hold values from -6 to 6
- cotangent: bfloat16 [4, 384, 15, 1024], P(None, 'dp'), may hold values from -6 to 6
- domain_ids: int32 [4, 384], P(None, 'dp'), may hold values from 0 to 6
- domain_counts: int32 [7], replicated, may hold values from 32 to 2047
- w_query: bfloat16 [1024, 1024], P('dp', 'mp'), may hold values from -0.25 to 0.25
- w_key: bfloat16 [1024, 1024], P('dp', 'mp'), may hold values from -0.25 to 0.25
- w_value: bfloat16 [1024, 1024], P('dp', 'mp'), may hold values from -0.1875 to 0.1875
- w_out: bfloat16 [1024, 1024], P('dp', 'mp'), may hold values from -0.375 to 0.375
- w_up: bfloat16 [1024, 2048], P('dp', 'mp'), may hold values from -0.1875 to 0.1875
- w_down: bfloat16 [1024, 2048], P('dp', 'mp'), may hold values from -0.125 to 0.125
- gain_attn: bfloat16 [1024], P('dp'), may hold values from 0.5 to 1.5
- shift_attn: bfloat16 [1024], P('dp'), may hold values from -3 to 3
- gain_ffn: bfloat16 [1024], P('dp'), may hold values from 0.5 to 1.5
- shift_ffn: bfloat16 [1024], P('dp'), may hold values from -3 to 3
Outputs:
- block_out: bfloat16 [4, 384, 15, 1024], P(None, 'dp')
- grad_tokens: float32 [4, 384, 15, 1024], P(None, 'dp')
- grad_query: float32 [1024, 1024], P('dp', 'mp')
- grad_key: float32 [1024, 1024], P('dp', 'mp')
- grad_value: float32 [1024, 1024], P('dp', 'mp')
- grad_out: float32 [1024, 1024], P('dp', 'mp')
- grad_up: float32 [1024, 2048], P('dp', 'mp')
- grad_down: float32 [1024, 2048], P('dp', 'mp')
- grad_gain_attn: float32 [1024], P('dp')
- grad_shift_attn: float32 [1024], P('dp')
- grad_gain_ffn: float32 [1024], P('dp')
- grad_shift_ffn: float32 [1024], P('dp')
All inputs are finite; a program needn't handle non-finite values.
Results may differ from a plain program's by a relative error of at most 0.013.
Values may be sent and summed in bfloat16 or wider, within the bound.
A program may use at most 192 MiB of HBM per device.

v0:
```python
import jax
import jax.numpy as jnp
from jax import lax
from jax.sharding import PartitionSpec as P

HD = 128


eps = 1e-05


def layer_norm(values, gain, shift):
    center = values - jnp.mean(values, axis=-1, keepdims=True)
    second = jnp.mean(center * center, axis=-1, keepdims=True)
    return center * lax.rsqrt(second + eps) * gain + shift


def exact_gelu(values):
    return jax.nn.gelu(values, approximate=False)


def collect(shards):
    return (
        lax.all_gather(shards[0], "dp", axis=0, tiled=True),
        lax.all_gather(shards[1], "dp", axis=0, tiled=True),
        lax.all_gather(shards[2], "dp", axis=0, tiled=True),
        lax.all_gather(shards[3], "dp", axis=0, tiled=True),
        lax.all_gather(shards[4], "dp", axis=0, tiled=True),
        lax.all_gather(shards[5], "dp", axis=0, tiled=True),
        lax.all_gather(shards[6], "dp", axis=0, tiled=True),
        lax.all_gather(shards[7], "dp", axis=0, tiled=True),
        lax.all_gather(shards[8], "dp", axis=0, tiled=True),
        lax.all_gather(shards[9], "dp", axis=0, tiled=True),
    )


def spread(grads):
    return (
        lax.psum_scatter(grads[0], "dp", scatter_dimension=0, tiled=True),
        lax.psum_scatter(grads[1], "dp", scatter_dimension=0, tiled=True),
        lax.psum_scatter(grads[2], "dp", scatter_dimension=0, tiled=True),
        lax.psum_scatter(grads[3], "dp", scatter_dimension=0, tiled=True),
        lax.psum_scatter(grads[4], "dp", scatter_dimension=0, tiled=True),
        lax.psum_scatter(grads[5], "dp", scatter_dimension=0, tiled=True),
        lax.psum_scatter(grads[6], "dp", scatter_dimension=0, tiled=True),
        lax.psum_scatter(grads[7], "dp", scatter_dimension=0, tiled=True),
        lax.psum_scatter(grads[8], "dp", scatter_dimension=0, tiled=True),
        lax.psum_scatter(grads[9], "dp", scatter_dimension=0, tiled=True),
    )


def one_batch(inputs, grad_in, gathered):
    w_query, w_key, w_value, w_out, w_up, w_down, gain_attn, shift_attn, gain_ffn, shift_ffn = (
        gathered
    )
    series, patches, width = inputs.shape
    row_count = series * patches
    local_heads = w_query.shape[1] // HD
    head_cols = local_heads * HD
    scale_factor = HD ** (-0.5)
    causal = jnp.arange(patches)[:, None] >= jnp.arange(patches)[None, :]

    def soft_weights(scores):
        return jax.nn.softmax(jnp.where(causal, scores, -1e30), axis=-1)

    flat_in = inputs.reshape(row_count, width).astype(jnp.float32)
    normed, norm_one_pull = jax.vjp(
        layer_norm, flat_in, gain_attn.astype(jnp.float32), shift_attn.astype(jnp.float32)
    )
    normed_low = normed.astype(jnp.bfloat16)

    def project(matrix):
        product = jnp.dot(normed_low, matrix, preferred_element_type=jnp.float32)
        return product.astype(jnp.bfloat16).reshape(series, patches, local_heads, HD)

    queries = project(w_query)
    keys_low = project(w_key)
    values_low = project(w_value)
    scores = (
        jnp.einsum("sihd,sjhd->shij", queries, keys_low, preferred_element_type=jnp.float32)
        * scale_factor
    )
    attention, soft_pull = jax.vjp(soft_weights, scores)
    attention_low = attention.astype(jnp.bfloat16)
    mixture = jnp.einsum(
        "shij,sjhd->sihd", attention_low, values_low, preferred_element_type=jnp.float32
    )
    mixture = mixture.astype(jnp.bfloat16).reshape(row_count, head_cols)
    attended = lax.psum(
        jnp.einsum("re,de->rd", mixture, w_out, preferred_element_type=jnp.float32), "mp"
    )
    residual = flat_in + attended
    normed_two, norm_two_pull = jax.vjp(
        layer_norm, residual, gain_ffn.astype(jnp.float32), shift_ffn.astype(jnp.float32)
    )
    normed_two_low = normed_two.astype(jnp.bfloat16)
    hidden = jnp.dot(normed_two_low, w_up, preferred_element_type=jnp.float32)
    active, gelu_pull = jax.vjp(exact_gelu, hidden)
    active_low = active.astype(jnp.bfloat16)
    ffn_out = lax.psum(
        jnp.einsum("rf,df->rd", active_low, w_down, preferred_element_type=jnp.float32).astype(
            jnp.bfloat16
        ),
        "mp",
    ).astype(jnp.float32)
    block_rows = (residual + ffn_out).astype(jnp.bfloat16).reshape(series, patches, width)
    grad_rows = grad_in.reshape(row_count, width)
    grad_low = grad_rows.astype(jnp.bfloat16)
    grad_down = jnp.einsum("rd,rf->df", grad_low, active_low, preferred_element_type=jnp.float32)
    grad_active = jnp.einsum("rd,df->rf", grad_low, w_down, preferred_element_type=jnp.float32)
    grad_hidden = gelu_pull(grad_active)[0].astype(jnp.bfloat16)
    grad_up = jnp.einsum(
        "rd,rf->df", normed_two_low, grad_hidden, preferred_element_type=jnp.float32
    )
    grad_normed_two = lax.psum(
        jnp.einsum("rf,df->rd", grad_hidden, w_up, preferred_element_type=jnp.float32), "mp"
    )
    grad_through_two, grad_gain_ffn, grad_shift_ffn = norm_two_pull(grad_normed_two)
    grad_residual = grad_rows + grad_through_two
    grad_att_low = grad_residual.astype(jnp.bfloat16)
    grad_out = jnp.einsum("rd,re->de", grad_att_low, mixture, preferred_element_type=jnp.float32)
    grad_mixture = jnp.einsum("rd,de->re", grad_att_low, w_out, preferred_element_type=jnp.float32)
    grad_mixture = grad_mixture.astype(jnp.bfloat16).reshape(series, patches, local_heads, HD)
    grad_attention = jnp.einsum(
        "sihd,sjhd->shij", grad_mixture, values_low, preferred_element_type=jnp.float32
    )
    grad_values = jnp.einsum(
        "shij,sihd->sjhd", attention_low, grad_mixture, preferred_element_type=jnp.float32
    ).astype(jnp.bfloat16)
    grad_scores = soft_pull(grad_attention)[0].astype(jnp.bfloat16)
    grad_queries = (
        jnp.einsum("shij,sjhd->sihd", grad_scores, keys_low, preferred_element_type=jnp.float32)
        * scale_factor
    ).astype(jnp.bfloat16)
    grad_keys = (
        jnp.einsum("shij,sihd->sjhd", grad_scores, queries, preferred_element_type=jnp.float32)
        * scale_factor
    ).astype(jnp.bfloat16)
    flat_queries = grad_queries.reshape(row_count, head_cols)
    flat_keys = grad_keys.reshape(row_count, head_cols)
    flat_values = grad_values.reshape(row_count, head_cols)
    grad_query = jnp.einsum(
        "rd,re->de", normed_low, flat_queries, preferred_element_type=jnp.float32
    )
    grad_key = jnp.einsum("rd,re->de", normed_low, flat_keys, preferred_element_type=jnp.float32)
    grad_value = jnp.einsum(
        "rd,re->de", normed_low, flat_values, preferred_element_type=jnp.float32
    )
    normed_terms = jnp.einsum(
        "re,de->rd", flat_queries, w_query, preferred_element_type=jnp.float32
    )
    normed_terms = normed_terms + jnp.einsum(
        "re,de->rd", flat_keys, w_key, preferred_element_type=jnp.float32
    )
    normed_terms = normed_terms + jnp.einsum(
        "re,de->rd", flat_values, w_value, preferred_element_type=jnp.float32
    )
    grad_normed = lax.psum(normed_terms.astype(jnp.bfloat16), "mp").astype(jnp.float32)
    grad_through_one, grad_gain_attn, grad_shift_attn = norm_one_pull(grad_normed)
    grad_inputs = (grad_residual + grad_through_one).reshape(series, patches, width)
    grads = (
        grad_query,
        grad_key,
        grad_value,
        grad_out,
        grad_up,
        grad_down,
        grad_gain_attn,
        grad_shift_attn,
        grad_gain_ffn,
        grad_shift_ffn,
    )
    return (block_rows, grad_inputs, grads)


def body(
    tokens,
    cotangent,
    domain_ids,
    domain_counts,
    w_query,
    w_key,
    w_value,
    w_out,
    w_up,
    w_down,
    gain_attn,
    shift_attn,
    gain_ffn,
    shift_ffn,
):
    shards = (
        w_query,
        w_key,
        w_value,
        w_out,
        w_up,
        w_down,
        gain_attn,
        shift_attn,
        gain_ffn,
        shift_ffn,
    )
    counts_real = domain_counts.astype(jnp.float32)
    mean_count = jnp.mean(counts_real)
    matches = (
        domain_ids[:, :, None] == jnp.arange(counts_real.shape[0], dtype=jnp.int32)[None, None, :]
    ).astype(jnp.float32)
    series_counts = jnp.sum(matches * counts_real, axis=-1)
    series_weight = 2.0 * mean_count / (mean_count + series_counts)
    outputs = []
    input_grads = []
    totals = None
    for micro_step in range(tokens.shape[0]):
        gathered = collect(shards)
        weighted = (
            cotangent[micro_step].astype(jnp.float32) * series_weight[micro_step][:, None, None]
        )
        block_rows, grad_inputs, grads = one_batch(tokens[micro_step], weighted, gathered)
        grads = spread(grads)
        totals = grads if totals is None else jax.tree.map(jnp.add, totals, grads)
        outputs.append(block_rows)
        input_grads.append(grad_inputs)
    return (jnp.stack(outputs), jnp.stack(input_grads)) + tuple(totals)


def solution(mesh):
    in_specs = (
        P(None, "dp", None, None),
        P(None, "dp", None, None),
        P(None, "dp"),
        P(),
        P("dp", "mp"),
        P("dp", "mp"),
        P("dp", "mp"),
        P("dp", "mp"),
        P("dp", "mp"),
        P("dp", "mp"),
        P("dp"),
        P("dp"),
        P("dp"),
        P("dp"),
    )
    out_specs = (
        P(None, "dp", None, None),
        P(None, "dp", None, None),
        P("dp", "mp"),
        P("dp", "mp"),
        P("dp", "mp"),
        P("dp", "mp"),
        P("dp", "mp"),
        P("dp", "mp"),
        P("dp"),
        P("dp"),
        P("dp"),
        P("dp"),
    )
    return jax.shard_map(body, mesh=mesh, in_specs=in_specs, out_specs=out_specs, check_vma=False)
```

profile of v0, /device:TPU:0, one launch (start us, length us, event | category | flops | bytes accessed | tf_op | source)
XLA Modules:
  0.0 1252.3 jit_solution(14896615397115699683)
XLA Ops:
  23.3 35.6 %all-reduce.11 = (bf16[1024]{0:T(1024)(128)(2,1)S(1)}, bf16[1024]{0:T(1024)(128)(2,1)S(1)}, bf16[1024]{0:T(1024)(128)(2,1)S(1)}, bf16[1024]{0:T(1024)(128)(2,1)S(1)}) all-reduce(bf16[1024]{0:T(1024)(128)(2,1)S(1)} %dynamic-update-slice.1, bf16[1024]{0:T(1024)(128)(2,1)S(1)} %dynamic-update-slice, ...), channel_id=1, replica_groups=mesh['dp'=16,'mp'=2] {'dp'}, use_global_device_ids=true, to_apply=%add.1 | all-reduce | flops 4096 | bytes 16384
  59.4 3.4 copy.238
  68.2 3.9 copy.254
  74.9 3.5 copy.262
  81.2 3.8 add_convert_fusion.23
  94.4 34.6 %all-gather.7.cloned.1.call-done = bf16[1024,512]{1,0:T(8,128)(2,1)} async-done(((bf16[64,512]{1,0:T(8,128)(2,1)}), bf16[1024,512]{1,0:T(8,128)(2,1)}) %all-gather.7.cloned.1.call-update) | async-done | bytes 1048592 | tf_op jit(solution)/shard_map/all_gather | solution.py:26
  210.9 124.2 %all-reduce.19.cloned.1.call-done = (f32[360,1024]{1,0:T(8,128)}, f32[360,1024]{1,0:T(8,128)}, f32[360,1024]{1,0:T(8,128)}, f32[360,1024]{1,0:T(8,128)}) async-done(((f32[360,1024]{1,0:T(8,128)}, f32[360,1024]{1,0:T(8,128)}, f32[360,1024]{1,0:T(8,128)}, f32[360,1024]{1,0:T(8,128)}), (f32[360,1024]{1,0:T(8,128)}, f32[360,1024]{1,0:T(8,128)}, f32[360,1024]{1,0:T(8,128)}, ...) | async-done | bytes 5898256 | tf_op jit(solution)/shard_map/psum | solution.py:89
  342.3 36.3 %all-gather.15.cloned.1.call-done = bf16[1024,1024]{1,0:T(8,128)(2,1)} async-done(((bf16[64,1024]{1,0:T(8,128)(2,1)}), bf16[1024,1024]{1,0:T(8,128)(2,1)}) %all-gather.15.cloned.1.call-update) | async-done | bytes 2097168 | tf_op jit(solution)/shard_map/all_gather | solution.py:28
  378.6 7.0 multiply_convert_fusion.3
  385.6 35.4 %all-gather.17.cloned.1.call-done = bf16[1024,1024]{1,0:T(8,128)(2,1)} async-done(((bf16[64,1024]{1,0:T(8,128)(2,1)}), bf16[1024,1024]{1,0:T(8,128)(2,1)}) %all-gather.17.cloned.1.call-update) | async-done | bytes 2097168 | tf_op jit(solution)/shard_map/all_gather | solution.py:29
  421.0 4.3 add_convert_fusion.11
  428.3 5.0 multiply_convert_fusion.2
  436.8 5.0 multiply_convert_fusion.1
  445.4 5.2 multiply_convert_fusion
  457.6 4.2 convolution_convert_fusion.3
  467.4 131.3 %all-reduce.17.cloned.1.call-done = (f32[360,1024]{1,0:T(8,128)}, f32[360,1024]{1,0:T(8,128)}, f32[360,1024]{1,0:T(8,128)}, f32[360,1024]{1,0:T(8,128)}) async-done(((f32[360,1024]{1,0:T(8,128)}, f32[360,1024]{1,0:T(8,128)}, f32[360,1024]{1,0:T(8,128)}, f32[360,1024]{1,0:T(8,128)}), (f32[360,1024]{1,0:T(8,128)}, f32[360,1024]{1,0:T(8,128)}, f32[360,1024]{1,0:T(8,128)}, ...) | async-done | bytes 5898256 | tf_op jit(solution)/shard_map/psum | solution.py:115
  601.8 6.7 multiply_reduce_fusion.3
  608.6 3.3 fusion.238
  694.2 3.7 add_add_fusion
  704.6 3.8 add_add_fusion.1
  716.7 3.7 add_convert_fusion
  759.8 72.0 %all-reduce.21.cloned.1.call-done = (bf16[360,1024]{1,0:T(8,128)(2,1)}, bf16[360,1024]{1,0:T(8,128)(2,1)}, bf16[360,1024]{1,0:T(8,128)(2,1)}, bf16[360,1024]{1,0...) async-done(((bf16[360,1024]{1,0:T(8,128)(2,1)}, bf16[360,1024]{1,0:T(8,128)(2,1)}, ...) | async-done | bytes 5898256 | tf_op jit(solution)/shard_map/psum | solution.py:100
  834.1 4.0 convert_reduce_fusion.3
  845.1 62.0 %all-reduce.8 = (f32[1024]{0:T(1024)S(1)}, f32[1024]{0:T(1024)S(1)}, f32[1024]{0:T(1024)S(1)}, f32[1024]{0:T(1024)S(1)}) all-reduce(f32[1024]{0:T(1024)S(1)} %add_add_fusion.25, f32[1024]{0:T(1024)S(1)} %add_add_fusion.24, f32[1024]{0:T(1024)S(1)} %add_add_fusion.23, ...), channel_id=38, replica_groups=mesh['dp'=16,'mp'=2] {'dp'}, use_global_device_ids=true, to_apply=%region_87.88.clone | all-reduce | flops 4096 | bytes 32768
  909.5 3.6 add_add_fusion.18
  924.1 3.4 pad_maximum_fusion
  927.5 6.0 copy.315
  954.7 30.9 %reduce-scatter.15.cloned.1.call-done = f32[64,1024]{1,0:T(8,128)} async-done(((f32[1024,1024]{1,0:T(8,128)}), f32[64,1024]{1,0:T(8,128)}) %reduce-scatter.15.cloned.1.call-update) | async-done | bytes 262160 | tf_op jit(solution)/shard_map/reduce_scatter | solution.py:43
  985.7 65.0 %reduce-scatter.13.cloned.1.call-done = f32[64,512]{1,0:T(8,128)} async-done(((f32[1024,512]{1,0:T(8,128)}), f32[64,512]{1,0:T(8,128)}) %reduce-scatter.13.cloned.1.call-update) | async-done | bytes 131088 | tf_op jit(solution)/shard_map/reduce_scatter | solution.py:42
  1050.6 65.1 %reduce-scatter.11.cloned.1.call-done = f32[64,512]{1,0:T(8,128)} async-done(((f32[1024,512]{1,0:T(8,128)}), f32[64,512]{1,0:T(8,128)}) %reduce-scatter.11.cloned.1.call-update) | async-done | bytes 131088 | tf_op jit(solution)/shard_map/reduce_scatter | solution.py:41
  1115.7 64.9 %reduce-scatter.9.cloned.1.call-done = f32[64,512]{1,0:T(8,128)} async-done(((f32[1024,512]{1,0:T(8,128)}), f32[64,512]{1,0:T(8,128)}) %reduce-scatter.9.cloned.1.call-update) | async-done | bytes 131088 | tf_op jit(solution)/shard_map/reduce_scatter | solution.py:40
  1180.6 64.9 %reduce-scatter.7.cloned.1.call-done = f32[64,512]{1,0:T(8,128)} async-done(((f32[1024,512]{1,0:T(8,128)}), f32[64,512]{1,0:T(8,128)}) %reduce-scatter.7.cloned.1.call-update) | async-done | bytes 131088 | tf_op jit(solution)/shard_map/reduce_scatter | solution.py:39
  (774 shorter events, 326.6 us)
Async XLA Ops:
  7.2 77.9 %all-gather.9.cloned.1.call-start = ((), (), s32[]{:S(2)}) async-start(), calls=%async_computation.7 | async-start | bytes 1114112 | tf_op jit(solution)/shard_map/all_gather | solution.py:24
  7.9 82.1 %all-gather.11.cloned.1.call-start = ((), (), s32[]{:S(2)}) async-start(), calls=%async_computation.8 | async-start | bytes 1114112 | tf_op jit(solution)/shard_map/all_gather | solution.py:25
  8.7 120.3 %all-gather.7.cloned.1.call-start = ((), (), s32[]{:S(2)}) async-start(), calls=%async_computation.6 | async-start | bytes 1114112 | tf_op jit(solution)/shard_map/all_gather | solution.py:26
  9.4 173.2 %all-gather.13.cloned.1.call-start = ((), (), s32[]{:S(2)}) async-start(), calls=%async_computation.9 | async-start | bytes 1114112 | tf_op jit(solution)/shard_map/all_gather | solution.py:27
  10.0 325.1 %all-reduce.19.cloned.1.call-start = ((), (), s32[]{:S(2)}) async-start(), calls=%async_computation.19 | async-start | bytes 11796480 | tf_op jit(solution)/shard_map/psum | solution.py:89
  16.7 161.4 %copy-start.219 = (pred[15,15]{0,1:T(8,128)(4,1)}, pred[15,15]{0,1:T(8,128)(4,1)S(1)}, u32[]{:S(2)}) copy-start(pred[15,15]{0,1:T(8,128)(4,1)S(1)} %iota_compare_fusion.1) | copy-start | bytes 679
  18.1 63.0 %copy-start.189 = (f32[360]{0:T(512)}, f32[360]{0:T(512)S(1)}, u32[]{:S(2)}) copy-start(f32[360]{0:T(512)S(1)} %rsqrt.92) | copy-start | bytes 4324
  191.3 187.4 %all-gather.15.cloned.1.call-start = ((), (), s32[]{:S(2)}) async-start(), calls=%async_computation.10 | async-start | bytes 2228224 | tf_op jit(solution)/shard_map/all_gather | solution.py:28
  191.8 229.1 %all-gather.17.cloned.1.call-start = ((), (), s32[]{:S(2)}) async-start(), calls=%async_computation.11 | async-start | bytes 2228224 | tf_op jit(solution)/shard_map/all_gather | solution.py:29
  192.6 406.0 %all-reduce.17.cloned.1.call-start = ((), (), s32[]{:S(2)}) async-start(), calls=%async_computation.18 | async-start | bytes 11796480 | tf_op jit(solution)/shard_map/psum | solution.py:115
  194.9 417.1 %copy-start.183 = (f32[360]{0:T(512)}, f32[360]{0:T(512)S(1)}, u32[]{:S(2)}) copy-start(f32[360]{0:T(512)S(1)} %mul.828) | copy-start | bytes 4324
  199.7 437.7 %copy-start.185 = (f32[360]{0:T(512)}, f32[360]{0:T(512)S(1)}, u32[]{:S(2)}) copy-start(f32[360]{0:T(512)S(1)} %mul.858) | copy-start | bytes 4324
  203.4 424.7 %copy-start.187 = (f32[360]{0:T(512)}, f32[360]{0:T(512)S(1)}, u32[]{:S(2)}) copy-start(f32[360]{0:T(512)S(1)} %mul.888) | copy-start | bytes 4324
  207.2 411.3 %copy-start.201 = (f32[360]{0:T(512)}, f32[360]{0:T(512)S(1)}, u32[]{:S(2)}) copy-start(f32[360]{0:T(512)S(1)} %mul.918) | copy-start | bytes 4324
  340.7 267.9 %copy-start.161 = (f32[360]{0:T(512)}, f32[360]{0:T(512)S(1)}, u32[]{:S(2)}) copy-start(f32[360]{0:T(512)S(1)} %broadcast_multiply_fusion.5) | copy-start | bytes 4324
  341.0 260.8 %copy-start.171 = (f32[360]{0:T(512)}, f32[360]{0:T(512)S(1)}, u32[]{:S(2)}) copy-start(f32[360]{0:T(512)S(1)} %broadcast_multiply_fusion.4) | copy-start | bytes 4324
  342.3 266.3 %copy-start.175 = (f32[360]{0:T(512)}, f32[360]{0:T(512)S(1)}, u32[]{:S(2)}) copy-start(f32[360]{0:T(512)S(1)} %fusion.212) | copy-start | bytes 4324
  342.3 266.3 %copy-start.177 = (f32[360]{0:T(512)}, f32[360]{0:T(512)S(1)}, u32[]{:S(2)}) copy-start(f32[360]{0:T(512)S(1)} %fusion.213) | copy-start | bytes 4324
  342.3 266.3 %copy-start.173 = (f32[360]{0:T(512)}, f32[360]{0:T(512)S(1)}, u32[]{:S(2)}) copy-start(f32[360]{0:T(512)S(1)} %fusion.214) | copy-start | bytes 4324
  342.3 259.4 %copy-start.199 = (f32[360]{0:T(512)}, f32[360]{0:T(512)S(1)}, u32[]{:S(2)}) copy-start(f32[360]{0:T(512)S(1)} %fusion.215) | copy-start | bytes 4324
  455.0 376.8 %all-reduce.21.cloned.1.call-start = ((), (), s32[]{:S(2)}) async-start(), calls=%async_computation.20 | async-start | bytes 11796480 | tf_op jit(solution)/shard_map/psum | solution.py:100
  686.8 267.9 %reduce-scatter.17.cloned.1.call-start = ((), (), s32[]{:S(2)}) async-start(), calls=%async_computation.17 | async-start | bytes 4456448 | tf_op jit(solution)/shard_map/reduce_scatter | solution.py:44
  697.9 287.7 %reduce-scatter.15.cloned.1.call-start = ((), (), s32[]{:S(2)}) async-start(), calls=%async_computation.16 | async-start | bytes 4456448 | tf_op jit(solution)/shard_map/reduce_scatter | solution.py:43
  708.4 342.2 %reduce-scatter.13.cloned.1.call-start = ((), (), s32[]{:S(2)}) async-start(), calls=%async_computation.15 | async-start | bytes 2228224 | tf_op jit(solution)/shard_map/reduce_scatter | solution.py:42
  716.0 399.7 %reduce-scatter.11.cloned.1.call-start = ((), (), s32[]{:S(2)}) async-start(), calls=%async_computation.14 | async-start | bytes 2228224 | tf_op jit(solution)/shard_map/reduce_scatter | solution.py:41
  744.6 436.0 %reduce-scatter.9.cloned.1.call-start = ((), (), s32[]{:S(2)}) async-start(), calls=%async_computation.13 | async-start | bytes 2228224 | tf_op jit(solution)/shard_map/reduce_scatter | solution.py:40
  751.3 494.2 %reduce-scatter.7.cloned.1.call-start = ((), (), s32[]{:S(2)}) async-start(), calls=%async_computation.12 | async-start | bytes 2228224 | tf_op jit(solution)/shard_map/reduce_scatter | solution.py:39
  759.1 72.7 %copy-start.168 = (f32[360]{0:T(512)S(1)}, f32[360]{0:T(512)}, u32[]{:S(2)}) copy-start(f32[360]{0:T(512)} %copy-done.167) | copy-start | bytes 4324
  759.1 74.9 %copy-start.208 = (f32[360]{0:T(512)S(1)}, f32[360]{0:T(512)}, u32[]{:S(2)}) copy-start(f32[360]{0:T(512)} %copy-done.207) | copy-start | bytes 4324
  759.1 74.9 %copy-start.164 = (f32[360]{0:T(512)S(1)}, f32[360]{0:T(512)}, u32[]{:S(2)}) copy-start(f32[360]{0:T(512)} %copy-done.163) | copy-start | bytes 4324
  759.1 74.9 %copy-start.166 = (f32[360]{0:T(512)S(1)}, f32[360]{0:T(512)}, u32[]{:S(2)}) copy-start(f32[360]{0:T(512)} %copy-done.165) | copy-start | bytes 4324
  759.1 74.9 %copy-start.182 = (f32[360]{0:T(512)S(1)}, f32[360]{0:T(512)}, u32[]{:S(2)}) copy-start(f32[360]{0:T(512)} %copy-done.181) | copy-start | bytes 4324
  (216 other events, 1102.4 us)
Sparse Core Ops, SparseCore 0:
  10.1 40.6 all-gather.8
  53.0 36.8 all-gather.10
  92.2 36.7 all-gather.6
  131.0 36.8 all-gather.12
  191.4 143.6 all-reduce.18
  337.1 41.4 all-gather.14
  380.8 40.1 all-gather.16
  455.1 143.4 all-reduce.16
  686.9 144.8 all-reduce.20
  836.0 73.3 reduce-scatter.16
  913.9 71.7 reduce-scatter.14
  989.8 60.7 reduce-scatter.12
  1054.9 60.7 reduce-scatter.10
  1119.9 60.6 reduce-scatter.8
  1184.8 60.7 reduce-scatter.6
where the time goes:
time: 1260 us; the launch traced here: 1250 us
  waiting for transfers between devices  731 us (58%)
  matrix products  186 us (15%)
  local copies, waits for them, and re-layouts  132 us (10%)
  blocking collectives  97.6 us (8%)
  other arithmetic  84 us (7%)
  between operations  19.8 us (2%)
    psum x1, waiting for transfers between devices, one_batch(): lax.psum(jnp.einsum('rf,df->rd', grad_hidden, w_up, preferred_element_typ...  131 us
    psum x1, waiting for transfers between devices, one_batch(): lax.psum(jnp.einsum('re,de->rd', mixture, w_out, preferred_element_type=j...  124 us
    unnamed x2, blocking collectives  97.6 us
    psum x1, waiting for transfers between devices, one_batch(): lax.psum(jnp.einsum('rf,df->rd', active_low, w_down, preferred_element_ty...  72 us
    reduce_scatter x1, waiting for transfers between devices, spread(): lax.psum_scatter(grads[2], 'dp', scatter_dimension=0, tiled=True)  65.1 us
    reduce_scatter x1, waiting for transfers between devices, spread(): lax.psum_scatter(grads[3], 'dp', scatter_dimension=0, tiled=True)  65 us
    reduce_scatter x1, waiting for transfers between devices, spread(): lax.psum_scatter(grads[0], 'dp', scatter_dimension=0, tiled=True)  64.9 us
    reduce_scatter x1, waiting for transfers between devices, spread(): lax.psum_scatter(grads[1], 'dp', scatter_dimension=0, tiled=True)  64.9 us
  transfers between devices with their start and end apart: 15, of which 12 were waited for; matrix products, arithmetic and copies ran while one was open for 21% of the time, Pallas kernels for 0%

commit v1 on v0

v1 whole, which is shorter than its diff:
```python
import functools

import jax
import jax.numpy as jnp
from jax import lax
from jax.experimental import pallas as pl
from jax.experimental.pallas import tpu as pltpu
from jax.sharding import PartitionSpec as P

BF = jnp.bfloat16
F32 = jnp.float32
HD = 128
SEG = 512
TILE = 128
PAD = 16
EPS = 1e-05
MESH = pl.DeviceIdType.MESH
VMEM_LIMIT = 62 * 1024 * 1024

Q, K, V, O, U0, U1, D0, D1 = range(8)
UPS = (U0, U1)
DOWNS = (D0, D1)
ORDERS = ("zxy", "zyx", "xyz", "zxy", "zyx", "xyz", "zxy", "zyx")


def nn(a, b):
    return lax.dot_general(a, b, (((1,), (0,)), ((), ())), preferred_element_type=F32)


def nt(a, b):
    return lax.dot_general(a, b, (((1,), (1,)), ((), ())), preferred_element_type=F32)


def flat(value):
    return value.reshape(-1, value.shape[-1])


def norm_stats(values):
    mean = jnp.mean(values, axis=-1, keepdims=True)
    center = values - mean
    inverse = lax.rsqrt(jnp.mean(center * center, axis=-1, keepdims=True) + EPS)
    return center * inverse, inverse


def norm_pull(grad, values, gain):
    normal, inverse = norm_stats(values)
    scaled = grad * gain
    first = jnp.mean(scaled, axis=-1, keepdims=True)
    second = jnp.mean(scaled * normal, axis=-1, keepdims=True)
    return inverse * (scaled - first - normal * second), normal


def fold_rows(values):
    rows, width = values.shape
    return jnp.sum(values.reshape(rows // 8, 8, width), axis=0)


def score_mask():
    row = lax.broadcasted_iota(jnp.int32, (TILE, TILE), 0)
    col = lax.broadcasted_iota(jnp.int32, (TILE, TILE), 1)
    return (row // PAD == col // PAD) & (col <= row)


def row_loop(rows, body, step=TILE):
    def once(index, carry):
        body(pl.ds(pl.multiple_of(index * step, step), step), index)
        return carry

    lax.fori_loop(0, rows // step, once, 0)


def half_loop(count, body):
    def once(index, carry):
        body(index)
        return carry

    lax.fori_loop(0, count, once, 0)


def half(index):
    return pl.ds(pl.multiple_of(index * SEG, SEG), SEG)


def norm_in(x, normed, gain, shift):
    def block(rows, _):
        normal, _inv = norm_stats(x[rows, :].astype(F32))
        normed[rows, :] = (normal * gain + shift).astype(BF)

    row_loop(x.shape[0], block)


def project(source, weights, seg, target):
    def one(m):
        target[:, half(m)] = nn(source[...], flat(weights[seg, m])).astype(BF)

    half_loop(weights.shape[1], one)


def attend(queries, keys, values, probs, mixture):
    mask = score_mask()
    scale = HD ** (-0.5)

    def group(rows, index):
        for head in range(queries.shape[1] // HD):
            cols = slice(head * HD, (head + 1) * HD)
            scores = nt(queries[rows, cols], keys[rows, cols]) * scale
            scores = jnp.where(mask, scores, -1e30)
            powers = jnp.exp(scores - jnp.max(scores, axis=-1, keepdims=True))
            share = powers * (1.0 / jnp.sum(powers, axis=-1, keepdims=True))
            probs[index, head] = share
            mixture[rows, cols] = nn(share.astype(BF), values[rows, cols]).astype(BF)

    row_loop(queries.shape[0], group)


def attend_back(queries, keys, values, probs, grad_mix, grad_q, grad_k, grad_v):
    scale = HD ** (-0.5)

    def group(rows, index):
        for head in range(queries.shape[1] // HD):
            cols = slice(head * HD, (head + 1) * HD)
            share = probs[index, head]
            grad = grad_mix[rows, cols]
            grad_share = nt(grad, values[rows, cols])
            grad_v[rows, cols] = nn(share.T.astype(BF), grad).astype(BF)
            inner = jnp.sum(grad_share * share, axis=-1, keepdims=True)
            grad_scores = share * (grad_share - inner)
            low = grad_scores.astype(BF)
            grad_q[rows, cols] = (nn(low, keys[rows, cols]) * scale).astype(BF)
            turned = grad_scores.T.astype(BF)
            grad_k[rows, cols] = (nn(turned, queries[rows, cols]) * scale).astype(BF)

    row_loop(queries.shape[0], group)


def back_through(source, weights, seg, total, fresh):
    def one(m):
        total[...] += nt(source(m), flat(weights[seg, m]))

    if fresh:
        total[...] = nt(source(0), flat(weights[seg, 0]))
        for m in range(1, weights.shape[1]):
            total[...] += nt(source(m), flat(weights[seg, m]))
    else:
        half_loop(weights.shape[1], one)


def feed_up(normed_two, weights, which, active, slope):
    def one(m):
        hidden = nn(normed_two[...], flat(weights[UPS[which], m]))
        bell = 0.5 + 0.5 * lax.erf(hidden * (0.5**0.5))
        active[which, m] = (hidden * bell).astype(BF)
        density = jnp.exp(-0.5 * hidden * hidden) * 0.3989422804014327
        slope[which, m] = bell + hidden * density

    half_loop(weights.shape[1], one)


def turn(source, target):
    def block(rows, _):
        target[:, rows] = source[rows, :].T

    row_loop(source.shape[0], block)


def weight_grad(turned, right, target, seg):
    def one(m):
        product = nn(turned[...], right(m)).astype(BF)
        target[seg, m] = product.reshape(target.shape[2:])

    half_loop(target.shape[1], one)


class Place:
    def __init__(self, shape):
        self.nz, self.nx, self.ny = shape
        index = lax.axis_index("dp")
        self.core = lax.rem(index, 2)
        chip = lax.div(index, 2)
        self.at = {"z": lax.div(chip, self.nx), "x": lax.rem(chip, self.nx), "y": lax.axis_index("mp")}
        self.count = {"z": self.nz, "x": self.nx, "y": self.ny}

    def device(self, core=None, **moved):
        at = {**self.at, **moved}
        core = self.core if core is None else core
        return ((at["z"] * self.nx + at["x"]) * 2 + core, at["y"])

    def partner(self):
        return self.device(core=1 - self.core)

    def neighbour(self, dim, step):
        return self.device(**{dim: self.at[dim] + step})

    def barrier(self, dims):
        semaphore = pltpu.get_barrier_semaphore()
        pl.semaphore_signal(semaphore, inc=1, device_id=self.partner(), device_id_type=MESH)
        peers = 1
        for dim in dims:
            for step in (1, -1):
                there = self.at[dim] + step
                valid = (there >= 0) & (there < self.count[dim])
                peers = peers + valid.astype(jnp.int32)

                @pl.when(valid)
                def _(dim=dim, step=step):
                    other = self.neighbour(dim, step)
                    pl.semaphore_signal(semaphore, inc=1, device_id=other, device_id_type=MESH)

        pl.semaphore_wait(semaphore, peers)


def link_slots(count, dims):
    return sum(2 * (count[dim] - 1) for dim in dims)


class Gather:
    def __init__(self, place, buffer, axes, order, sems):
        self.place, self.buffer, self.axes, self.order = place, buffer, axes, order
        self.send, self.recv, self.pass_send, self.pass_recv = sems
        self.rounds = [(dim, t) for dim in order for t in range(place.count[dim] - 1)]
        self.slots = {}
        for dim, t in self.rounds:
            for way in (1, -1):
                self.slots[dim, t, way] = len(self.slots)

    def block(self, dim, position, core):
        done = self.order[: self.order.index(dim)] if dim else ""
        index = []
        for axis in self.axes:
            if axis == dim:
                index.append(position)
            elif axis in done:
                index.append(pl.ds(0, self.place.count[axis]))
            else:
                index.append(self.place.at[axis])
        return self.buffer.at[tuple(index) + (core,)]

    def link(self, dim, t, way, position, device):
        block = self.block(dim, position, self.place.core)
        slot = self.slots[dim, t, way]
        return pltpu.make_async_remote_copy(
            block, block, self.send.at[slot], self.recv.at[slot], device_id=device, device_id_type=MESH
        )

    def hand(self, slot, dim, position, core):
        block = self.block(dim, position, core)
        return pltpu.make_async_remote_copy(
            block,
            block,
            self.pass_send.at[slot],
            self.pass_recv.at[slot],
            device_id=self.place.partner(),
            device_id_type=MESH,
        )

    def sends(self, dim, t):
        here, count = self.place.at[dim], self.place.count[dim]
        yield 1, here - t, (here - t >= 0) & (here < count - 1)
        yield -1, here + t, (here + t < count) & (here > 0)

    def arrivals(self, dim, t):
        here, count = self.place.at[dim], self.place.count[dim]
        yield 1, here - 1 - t, here - 1 - t >= 0
        yield -1, here + 1 + t, here + 1 + t < count

    def start(self):
        self.hand(len(self.slots), "", None, self.place.core).start()
        self.send_round(0)

    def send_round(self, number):
        dim, t = self.rounds[number]
        for way, position, valid in self.sends(dim, t):

            @pl.when(valid)
            def _(way=way, position=position):
                self.link(dim, t, way, position, self.place.neighbour(dim, way)).start()

    def advance(self, number):
        dim, t = self.rounds[number - 1]
        for way, position, valid in self.arrivals(dim, t):

            @pl.when(valid)
            def _(way=way, position=position):
                self.link(dim, t, way, position, self.place.partner()).wait_recv()
                self.hand(self.slots[dim, t, way], dim, position, self.place.core).start()

        if number < len(self.rounds):
            self.send_round(number)

    def finish(self):
        other = 1 - self.place.core
        self.hand(len(self.slots), "", None, other).wait_recv()
        for dim, t in self.rounds:
            for way, position, valid in self.arrivals(dim, t):

                @pl.when(valid)
                def _(dim=dim, t=t, way=way, position=position):
                    self.hand(self.slots[dim, t, way], dim, position, other).wait_recv()

    def drain(self):
        self.hand(len(self.slots), "", None, self.place.core).wait_send()
        for dim, t in self.rounds:
            for way, position, valid in self.sends(dim, t):

                @pl.when(valid)
                def _(dim=dim, t=t, way=way, position=position):
                    self.link(dim, t, way, position, self.place.partner()).wait_send()

            for way, position, valid in self.arrivals(dim, t):

                @pl.when(valid)
                def _(dim=dim, t=t, way=way, position=position):
                    self.hand(self.slots[dim, t, way], dim, position, self.place.core).wait_send()


class Scatter:
    def __init__(self, place, mine, axes, order, inbox, hand_box, sems, both=False):
        self.place, self.mine, self.axes, self.order, self.both = place, mine, axes, order, both
        self.inbox, self.hand_box = inbox, hand_box
        self.send, self.recv = sems
        self.rounds = [(dim, t) for dim in order for t in range(place.count[dim] - 1)]
        self.slots = {}
        for dim, t in self.rounds:
            for way in (1, -1):
                self.slots[dim, t, way] = len(self.slots) + 1

    def own(self, index):
        return index + ((() if self.both else (self.place.core,)))

    def hand(self):
        whole = tuple(pl.ds(0, self.place.count[axis]) for axis in self.axes)
        source = self.mine.at[whole] if self.both else self.mine.at[whole + (1 - self.place.core,)]
        return pltpu.make_async_remote_copy(
            source, self.hand_box, self.send.at[0], self.recv.at[0], device_id=self.place.partner(), device_id_type=MESH
        )

    def start(self):
        self.hand().start()

    def take_hand(self):
        self.hand().wait_recv()
        first = self.place.count[self.axes[0]]
        rest = tuple(pl.ds(0, self.place.count[axis]) for axis in self.axes[1:])
        if self.both:
            self.hand().wait_send()
            self.mine[...] = self.mine[...] + self.hand_box[...]
        else:
            for p in range(first):
                for r in range(self.place.count[self.axes[1]]):
                    index = (p, r) + rest[1:]
                    here = self.mine[index + (self.place.core,)].astype(F32)
                    there = self.hand_box[index].astype(F32)
                    self.mine[index + (self.place.core,)] = (here + there).astype(self.mine.dtype)
        self.send_round(0)

    def block(self, dim, position):
        done = self.order[: self.order.index(dim)]
        index = []
        for axis in self.axes:
            if axis == dim:
                index.append(position)
            elif axis in done:
                index.append(self.place.at[axis])
            else:
                index.append(pl.ds(0, self.place.count[axis]))
        return self.own(tuple(index))

    def link(self, dim, t, way, position, device):
        slot = self.slots[dim, t, way]
        return pltpu.make_async_remote_copy(
            self.mine.at[self.block(dim, position)],
            self.inbox[slot],
            self.send.at[slot],
            self.recv.at[slot],
            device_id=device,
            device_id_type=MESH,
        )

    def sends(self, dim, t):
        here, count = self.place.at[dim], self.place.count[dim]
        yield 1, count - 1 - t + here, (t >= here) & (here < count - 1)
        back = count - 1 - here
        yield -1, t - back, (t >= back) & (here > 0)

    def arrivals(self, dim, t):
        here, count = self.place.at[dim], self.place.count[dim]
        yield 1, count - 2 - t + here, (t >= here - 1) & (here > 0)
        back = count - 1 - here
        yield -1, t + 1 - back, (t >= back - 1) & (here < count - 1)

    def send_round(self, number):
        dim, t = self.rounds[number]
        for way, position, valid in self.sends(dim, t):

            @pl.when(valid)
            def _(way=way, position=position):
                self.link(dim, t, way, position, self.place.neighbour(dim, way)).start()

    def advance(self, number):
        dim, t = self.rounds[number - 1]
        for way, position, valid in self.arrivals(dim, t):

            @pl.when(valid)
            def _(way=way, position=position):
                self.link(dim, t, way, position, self.place.partner()).wait_recv()
                index = self.block(dim, position)
                total = self.mine[index].astype(F32) + self.inbox[self.slots[dim, t, way]][...].astype(F32)
                self.mine[index] = total.astype(self.mine.dtype)

        if number < len(self.rounds):
            self.send_round(number)

    def result(self):
        return self.mine[self.own(tuple(self.place.at[axis] for axis in self.axes))]

    def drain(self):
        if not self.both:
            self.hand().wait_send()
        for dim, t in self.rounds:
            for way, position, valid in self.sends(dim, t):

                @pl.when(valid)
                def _(dim=dim, t=t, way=way, position=position):
                    self.link(dim, t, way, position, self.place.partner()).wait_send()


def inbox_shapes(count, axes, order, block):
    shapes, left = [], dict(count)
    for dim in order:
        left.pop(dim)
        for _ in range(2 * (count[dim] - 1)):
            shapes.append(tuple(count[axis] for axis in axes if axis in left) + block)
    return shapes


def read_vectors(vectors, tiles):
    nz, nx = tiles.shape[:2]
    pieces = []
    for z in range(nz):
        for x in range(nx):
            pieces.append(tiles[z, x, 0].astype(F32) + tiles[z, x, 1].astype(F32))
    vectors[...] = jnp.concatenate(pieces, axis=1)[:8]


def forward_stages(x, vectors, g, nrm, q, k, v, probs, mix, res, nrm2, active, slope, block_out):
    gain, shift = vectors[0:1, :], vectors[1:2, :]
    gain_two, shift_two = vectors[2:3, :], vectors[3:4, :]
    norm_in(x, nrm, gain, shift)
    for seg, target in ((Q, q), (K, k), (V, v)):
        project(nrm, g, seg, target)
    attend(q, k, v, probs, mix)
    back_through(lambda m: mix[:, half(m)], g, O, res, True)

    def second(rows, _):
        total = res[rows, :] + x[rows, :].astype(F32)
        res[rows, :] = total
        normal, _inv = norm_stats(total)
        nrm2[rows, :] = (normal * gain_two + shift_two).astype(BF)

    row_loop(x.shape[0], second)
    for which in range(2):
        feed_up(nrm2, g, which, active, slope)


def forward_tail(g, res, active, block_out, total):
    for which in range(2):
        back_through(lambda m, which=which: active[which, m], g, DOWNS[which], total, which == 0)

    def last(rows, _):
        block_out[rows, :] = (res[rows, :] + total[rows, :]).astype(BF)

    row_loop(res.shape[0], last)


def forward_kernel(x, vectors, g, nrm, q, k, v, probs, mix, res, nrm2, active, slope, block_out, total):
    forward_stages(x, vectors, g, nrm, q, k, v, probs, mix, res, nrm2, active, slope, block_out)
    forward_tail(g, res, active, block_out, total)


def gather_kernel(shape, shards, tile, g_out, vectors, g, tiles, send, recv, pass_send, pass_recv, local):
    place = Place(shape)
    segs = shards.shape[0]
    mine = []
    for seg in range(segs):
        spot = g.at[seg, place.at["y"], place.at["z"], place.at["x"], place.core]
        copy = pltpu.make_async_copy(shards.at[seg], spot, local.at[seg])
        copy.start()
        mine.append(copy)
    spot = tiles.at[place.at["z"], place.at["x"], place.core]
    copy = pltpu.make_async_copy(tile, spot, local.at[segs])
    copy.start()
    mine.append(copy)
    place.barrier("zxy")
    runs = []
    for seg in range(segs):
        sems = tuple(sem.at[seg] for sem in (send, recv, pass_send, pass_recv))
        runs.append(Gather(place, g.at[seg], "yzx", ORDERS[seg], sems))
    sems = tuple(sem.at[segs] for sem in (send, recv, pass_send, pass_recv))
    runs.append(Gather(place, tiles, "zx", "zx", sems))
    order = [segs] + list(range(segs))
    for index in order:
        mine[index].wait()
        runs[index].start()
    deepest = max(len(run.rounds) for run in runs)
    for number in range(1, deepest + 1):
        for index in order:
            if number <= len(runs[index].rounds):
                runs[index].advance(number)
    for index in order:
        runs[index].finish()
    copy = pltpu.make_async_copy(g, g_out, local.at[segs + 1])
    copy.start()
    read_vectors(vectors, tiles)
    for index in order:
        runs[index].drain()
    copy.wait()


def fetch(source, target, sems, segs):
    copies = []
    for index, seg in enumerate(segs):
        copy = pltpu.make_async_copy(source.at[seg], target.at[index], sems.at[index])
        copy.start()
        copies.append(copy)
    return copies


def feed_back_kernel(cot, row_weight, vectors, g_all, active, slope, nrm2, res, dw, gres, vec, g, gl, glt, gh, n2t, gn2, sems):
    copies = fetch(g_all, g, sems, DOWNS + UPS)
    gain_two = vectors[2:3, :]

    def first(rows, _):
        gl[rows, :] = (cot[rows, :].astype(F32) * row_weight[rows, :]).astype(BF)

    row_loop(cot.shape[0], first)
    turn(gl, glt)
    turn(nrm2, n2t)
    for which in range(2):
        copies[which].wait()

        def one(m, which=which):
            pulled = nn(gl[...], flat(g[which, m]))
            gh[which, m] = (pulled * slope[which, m]).astype(BF)

        half_loop(g.shape[1], one)
        weight_grad(glt, lambda m, which=which: active[which, m], dw, 2 + which)
    for which in range(2):
        copies[2 + which].wait()
        weight_grad(n2t, lambda m, which=which: gh[which, m], dw, which)
        back_through(lambda m, which=which: gh[which, m], g, 2 + which, gn2, which == 0)
    vec[...] = jnp.zeros_like(vec)

    def last(rows, _):
        grad = gn2[rows, :]
        pulled, normal = norm_pull(grad, res[rows, :], gain_two)
        vec[0] += fold_rows(grad * normal)
        vec[1] += fold_rows(grad)
        gres[rows, :] = cot[rows, :].astype(F32) * row_weight[rows, :] + pulled

    row_loop(cot.shape[0], last)


def attn_back_kernel(
    gres, x, vectors, g_all, mix, probs, q, k, v, nrm, dw, gtok, vec, g, gal, galt, gm, gq, gk, gv, nrmt, gn, sems
):
    copies = fetch(g_all, g, sems, (O, Q, K, V))
    gain = vectors[0:1, :]

    def first(rows, _):
        gal[rows, :] = gres[rows, :].astype(BF)

    row_loop(x.shape[0], first)
    turn(gal, galt)
    turn(nrm, nrmt)
    copies[0].wait()
    project(gal, g, 0, gm)
    weight_grad(galt, lambda m: mix[:, half(m)], dw, 3)
    attend_back(q, k, v, probs, gm, gq, gk, gv)
    for seg, grad in ((0, gq), (1, gk), (2, gv)):
        copies[1 + seg].wait()
        weight_grad(nrmt, lambda m, grad=grad: grad[:, half(m)], dw, seg)
        back_through(lambda m, grad=grad: grad[:, half(m)], g, 1 + seg, gn, seg == 0)
    vec[...] = jnp.zeros_like(vec)

    def last(rows, _):
        grad = gn[rows, :]
        pulled, normal = norm_pull(grad, x[rows, :].astype(F32), gain)
        vec[0] += fold_rows(grad * normal)
        vec[1] += fold_rows(grad)
        gtok[rows, :] = gres[rows, :] + pulled

    row_loop(x.shape[0], last)


def vector_tiles(tiles, vec_a, vec_f):
    tiles[...] = jnp.zeros_like(tiles)
    nz, nx = tiles.shape[:2]
    for line, (source, part) in enumerate(((vec_a, 0), (vec_a, 1), (vec_f, 0), (vec_f, 1))):
        row = jnp.sum(source[part], axis=0, keepdims=True)
        for z in range(nz):
            for x in range(nx):
                chip = z * nx + x
                tiles[z, x, line : line + 1, :] = row[:, chip * 128 : (chip + 1) * 128]


def scatter_kernel(shape, plan, dw_a, dw_f, vec_a, vec_f, *refs):
    outs, vec_out = refs[:6], refs[6]
    dw, tiles, hands, vec_hand, ybox, local, send, recv, ysem = refs[7:16]
    boxes = refs[16:]
    place = Place(shape)
    loads = []
    for seg in (D0, D1, U0, U1, O, Q, K, V):
        source = dw_a.at[seg] if seg < 4 else dw_f.at[seg - 4]
        copy = pltpu.make_async_copy(source, dw.at[seg], local.at[seg])
        copy.start()
        loads.append((seg, copy))
    vector_tiles(tiles, vec_a, vec_f)
    place.barrier("zxy")
    segs = dw.shape[0]
    runs, start = {}, 0
    for seg in range(segs + 1):
        order = ORDERS[seg][::-1] if seg < segs else "zx"
        sems = (send.at[seg], recv.at[seg])
        if seg < segs:
            run = Scatter(place, dw.at[seg], "yzx", order, {}, hands.at[seg], sems)
        else:
            run = Scatter(place, tiles, "zx", "zx", {}, vec_hand, sems, both=True)
        for slot in range(1, len(run.slots) + 1):
            run.inbox[slot] = boxes[start + slot - 1]
        start += len(run.slots)
        runs[seg] = run
    runs[segs].start()
    line = [segs]
    for seg, copy in loads:
        copy.wait()
        runs[seg].start()
        line.append(seg)
    for index in line:
        runs[index].take_hand()
    deepest = max(len(run.rounds) for run in runs.values())
    for number in range(1, deepest + 1):
        for index in line:
            if number <= len(runs[index].rounds):
                runs[index].advance(number)
    here = tiles.at[place.at["z"], place.at["x"]]
    other = place.device(y=1 - place.at["y"])
    copy = pltpu.make_async_remote_copy(here, ybox, ysem.at[0], ysem.at[1], device_id=other, device_id_type=MESH)
    copy.start()
    for seg in range(4):
        outs[seg][...] = runs[seg].result().astype(F32)
    for which in range(2):
        outs[4][:, which * SEG : (which + 1) * SEG] = runs[UPS[which]].result().astype(F32)
        outs[5][:, which * SEG : (which + 1) * SEG] = runs[DOWNS[which]].result().astype(F32)
    copy.wait()
    vec_out[...] = tiles[place.at["z"], place.at["x"]] + ybox[...]
    for index in line:
        runs[index].drain()


def shape_of(shape, dtype):
    return jax.ShapeDtypeStruct(shape, dtype)


IN_VMEM = pl.BlockSpec(memory_space=pltpu.VMEM)
ANYWHERE = pl.BlockSpec(memory_space=pl.ANY)


def call(body, outs, ins, out_specs, scratch, name, collective=None):
    params = {"vmem_limit_bytes": VMEM_LIMIT}
    if collective is not None:
        params.update(collective_id=collective, has_side_effects=True)
    return pl.pallas_call(
        body,
        out_shape=outs,
        in_specs=ins,
        out_specs=out_specs,
        scratch_shapes=scratch,
        compiler_params=pltpu.CompilerParams(**params),
        name=name,
    )


def gather_weights(shape, shards, tile):
    nz, nx, ny = shape
    segs, rows, cols = shards.shape
    full = (segs, ny, nz, nx, 2, rows, cols)
    count = {"z": nz, "x": nx, "y": ny}
    slots = link_slots(count, "zxy")
    dma = pltpu.SemaphoreType.DMA
    scratch = [
        pltpu.VMEM(full, BF),
        pltpu.VMEM((nz, nx, 2) + tile.shape, BF),
        dma((segs + 1, slots)),
        dma((segs + 1, slots)),
        dma((segs + 1, slots + 1)),
        dma((segs + 1, slots + 1)),
        dma((segs + 2,)),
    ]
    outs = (shape_of(full, BF), shape_of((8, nz * nx * 128), F32))
    return call(
        functools.partial(gather_kernel, shape), outs, [IN_VMEM] * 2, (ANYWHERE, IN_VMEM), scratch, "gather_weights", 0
    )(shards, tile)


def forward(x, vectors, g):
    rows, width = x.shape
    heads, groups = width // HD, rows // TILE
    wide = (2, g.shape[1], rows, SEG)
    low = shape_of((rows, width), BF)
    outs = (
        low,
        low,
        low,
        low,
        shape_of((groups, heads, TILE, TILE), F32),
        low,
        shape_of((rows, width), F32),
        low,
        shape_of(wide, BF),
        shape_of(wide, F32),
        low,
    )
    scratch = [pltpu.VMEM((rows, width), F32)]
    return call(forward_kernel, outs, [IN_VMEM] * 3, (IN_VMEM,) * len(outs), scratch, "forward")(x, vectors, g)


def feed_back(cot, row_weight, vectors, g, active, slope, nrm2, res):
    rows, width = cot.shape
    part = (4,) + g.shape[1:]
    outs = (shape_of(part, BF), shape_of((rows, width), F32), shape_of((2, 8, width), F32))
    low = pltpu.VMEM((rows, width), BF)
    scratch = [
        pltpu.VMEM(part, BF),
        low,
        pltpu.VMEM((width, rows), BF),
        pltpu.VMEM(active.shape, BF),
        pltpu.VMEM((width, rows), BF),
        pltpu.VMEM((rows, width), F32),
        pltpu.SemaphoreType.DMA((4,)),
    ]
    ins = [IN_VMEM] * 8
    ins[3] = ANYWHERE
    return call(feed_back_kernel, outs, ins, (IN_VMEM,) * 3, scratch, "feed_back")(
        cot, row_weight, vectors, g, active, slope, nrm2, res
    )


def attn_back(gres, x, vectors, g, mix, probs, q, k, v, nrm):
    rows, width = x.shape
    part = (4,) + g.shape[1:]
    outs = (shape_of(part, BF), shape_of((rows, width), F32), shape_of((2, 8, width), F32))
    low = pltpu.VMEM((rows, width), BF)
    turned = pltpu.VMEM((width, rows), BF)
    scratch = [
        pltpu.VMEM(part, BF),
        low,
        turned,
        low,
        low,
        low,
        low,
        turned,
        pltpu.VMEM((rows, width), F32),
        pltpu.SemaphoreType.DMA((4,)),
    ]
    ins = [IN_VMEM] * 10
    ins[3] = ANYWHERE
    return call(attn_back_kernel, outs, ins, (IN_VMEM,) * 3, scratch, "attn_back")(
        gres, x, vectors, g, mix, probs, q, k, v, nrm
    )


def scatter_grads(shape, dw_a, dw_f, vec_a, vec_f):
    nz, nx, ny = shape
    rows, cols = dw_a.shape[-2:]
    segs = 8
    count = {"z": nz, "x": nx, "y": ny}
    slots = link_slots(count, "zxy")
    dma = pltpu.SemaphoreType.DMA
    full = (segs,) + dw_a.shape[1:]
    scratch = [
        pltpu.VMEM(full, BF),
        pltpu.VMEM((nz, nx, 8, 128), F32),
        pltpu.VMEM((segs, ny, nz, nx, rows, cols), BF),
        pltpu.VMEM((nz, nx, 8, 128), F32),
        pltpu.VMEM((8, 128), F32),
        dma((segs,)),
        dma((segs + 1, slots + 1)),
        dma((segs + 1, slots + 1)),
        dma((2,)),
    ]
    for seg in range(segs):
        scratch += [pltpu.VMEM(s, BF) for s in inbox_shapes(count, "yzx", ORDERS[seg][::-1], (rows, cols))]
    scratch += [pltpu.VMEM(s, F32) for s in inbox_shapes({"z": nz, "x": nx}, "zx", "zx", (8, 128))]
    small, large = shape_of((rows, cols), F32), shape_of((rows, 2 * cols), F32)
    outs = (small, small, small, small, large, large, shape_of((8, 128), F32))
    return call(
        functools.partial(scatter_kernel, shape, None),
        outs,
        [ANYWHERE, ANYWHERE, IN_VMEM, IN_VMEM],
        (IN_VMEM,) * 7,
        scratch,
        "scatter_grads",
        1,
    )(dw_a, dw_f, vec_a, vec_f)


def chip_grid(chips):
    nx = 1
    while (nx * 2) ** 2 <= chips:
        nx *= 2
    return chips // nx, nx


def body(counts_of, tokens, cotangent, domain_ids, domain_counts, *params):
    weights, norms = params[:6], params[6:]
    n_dp, n_mp = counts_of
    micro = tokens.shape[0] // n_mp
    y = lax.axis_index("mp")
    dp = lax.axis_index("dp")

    def mine(array):
        return lax.dynamic_slice_in_dim(array, y * micro, micro, 0)

    counts_real = domain_counts.astype(F32)
    mean_count = jnp.mean(counts_real)
    kinds = jnp.arange(counts_real.shape[0], dtype=jnp.int32)
    ids = mine(domain_ids)
    matches = (ids[:, :, None] == kinds).astype(F32)
    series_counts = jnp.sum(matches * counts_real, axis=-1)
    series_weight = 2.0 * mean_count / (mean_count + series_counts)
    series, patches, width = ids.shape[1], tokens.shape[2], tokens.shape[3]
    rows = micro * series * PAD
    row_weight = jnp.broadcast_to(series_weight[:, :, None], (micro, series, PAD)).reshape(rows, 1)

    def padded(array):
        return jnp.pad(mine(array), ((0, 0), (0, 0), (0, PAD - patches), (0, 0))).reshape(rows, width)

    x, cot = padded(tokens), padded(cotangent)
    wq, wk, wv, wo, wu, wd = weights
    shards = jnp.stack((wq, wk, wv, wo, wu[:, :SEG], wu[:, SEG:], wd[:, :SEG], wd[:, SEG:]))
    linked = shards.shape[1] % 16 == 0 and n_dp % 4 == 0 and shards.shape[1] * n_dp == width
    share = width // n_dp
    if linked:
        shape = chip_grid(n_dp // 2) + (n_mp,)
        core = lax.rem(dp, 2)
        tile = jnp.stack(norms)
        tile = jnp.where(core == 0, jnp.pad(tile, ((0, 12), (0, share))), jnp.pad(tile, ((0, 12), (share, 0))))
        g, vectors = gather_weights(shape, shards, tile)
    else:
        g = lax.all_gather(lax.all_gather(shards, "dp", axis=1, tiled=True), "mp", axis=1)
        vectors = lax.all_gather(jnp.stack(norms), "dp", axis=1, tiled=True).astype(F32)
        vectors = jnp.pad(vectors, ((0, 4), (0, 0)))
    nrm, q, k, v, probs, mix, res, nrm2, active, slope, block_out = forward(x, vectors, g)
    dw_f, gres, vec_f = feed_back(cot, row_weight, vectors, g, active, slope, nrm2, res)
    dw_a, gtok, vec_a = attn_back(gres, x, vectors, g, mix, probs, q, k, v, nrm)
    if linked:
        grads = scatter_grads(shape, dw_a, dw_f, vec_a, vec_f)
        grads, vec = list(grads[:6]), grads[6]
        vec = lax.dynamic_slice(vec, (0, core * share), (4, share))
    else:
        dw = jnp.concatenate((dw_a, dw_f)).astype(F32)
        dw = lax.psum_scatter(lax.psum_scatter(dw, "mp", scatter_dimension=1), "dp", scatter_dimension=1, tiled=True)
        grads = [dw[0], dw[1], dw[2], dw[3]]
        grads += [jnp.concatenate((dw[a], dw[b]), axis=1) for a, b in (UPS, DOWNS)]
        vec = jnp.concatenate((jnp.sum(vec_a, axis=1), jnp.sum(vec_f, axis=1)))
        vec = lax.psum_scatter(lax.psum(vec, "mp"), "dp", scatter_dimension=1, tiled=True)

    def both_halves(array):
        own = array.reshape(micro, series, PAD, width)[:, :, :patches]
        whole = jnp.zeros((micro * n_mp,) + own.shape[1:], own.dtype)
        whole = lax.dynamic_update_slice_in_dim(whole, own, y * micro, 0)
        piece, at = own, y
        for _ in range(n_mp - 1):
            piece = lax.ppermute(piece, "mp", [(i, (i + 1) % n_mp) for i in range(n_mp)])
            at = lax.rem(at + n_mp - 1, n_mp)
            whole = lax.dynamic_update_slice_in_dim(whole, piece, at * micro, 0)
        return whole

    out = both_halves(block_out)
    grad_tokens = both_halves(gtok)
    return (out, grad_tokens, *grads, vec[0], vec[1], vec[2], vec[3])


def solution(mesh):
    rows, matrix, vector = P(None, "dp", None, None), P("dp", "mp"), P("dp")
    in_specs = (rows, rows, P(None, "dp"), P()) + (matrix,) * 6 + (vector,) * 4
    out_specs = (rows, rows) + (matrix,) * 6 + (vector,) * 4
    run = functools.partial(body, (mesh.shape["dp"], mesh.shape["mp"]))
    return jax.shard_map(run, mesh=mesh, in_specs=in_specs, out_specs=out_specs, check_vma=False)
```

time: 1260 us -> 441 us (0.35)
  waiting for transfers between devices: 731 us -> 0.01 us
  Pallas kernels: 0 us -> 389 us
  matrix products: 186 us -> 0 us
  blocking collectives: 97.6 us -> 0 us
  local copies, waits for them, and re-layouts: 132 us -> 37 us
  other arithmetic: 84 us -> 2.7 us
  between operations: 19.8 us -> 2.61 us
    pallas_call x0 -> x5, Pallas kernels: none -> 389 us  [the longest x1 170 us: scatter_grads(): call(functools.partial(scatter_kernel, shape, None), outs, [ANYWHERE, ANY...]
    psum x3 -> x0, waiting for transfers between devices: 327 us -> none  [the longest x1 131 us: one_batch(): lax.psum(jnp.einsum('rf,df->rd', grad_hidden, w_up, preferred_element_typ...]
    reduce_scatter x6 -> x0, waiting for transfers between devices: 291 us -> none  [the longest x1 65.1 us: spread(): lax.psum_scatter(grads[2], 'dp', scatter_dimension=0, tiled=True)]
    dot_general x96 -> x0, matrix products: 186 us -> none  [the longest x12 27 us: project(): product = jnp.dot(normed_low, matrix, preferred_element_type=jnp.float32)]
    all_gather x6 -> x0, waiting for transfers between devices: 109 us -> none  [the longest x1 36.3 us: collect(): lax.all_gather(shards[4], 'dp', axis=0, tiled=True)]
    unnamed x2 -> x0, blocking collectives: 97.6 us -> none
    convert_element_type x40 -> x0, local copies, waits for them, and re-layouts: 56.9 us -> none  [the longest x8 21.6 us: one_batch(): flat_in = inputs.reshape(row_count, width).astype(jnp.float32)]
    reduce_sum x15 -> x0, other arithmetic: 31.3 us -> none  [the longest x6 19.8 us: layer_norm(): return center * lax.rsqrt(second + eps) * gain + shift]
  transfers between devices with their start and end apart: 15 -> 2, of which waited for: 12 -> 0; matrix products, arithmetic and copies ran while one was open for 21% -> 1% of each run, Pallas kernels for 0% -> 39%
where the time goes in v1:
time: 441 us; the launch traced here: 433 us
  Pallas kernels  389 us (88%)
  local copies, waits for them, and re-layouts  37 us (8%)
    pallas_call x1, Pallas kernels, scatter_grads(): call(functools.partial(scatter_kernel, shape, None), outs, [ANYWHERE, ANY...  170 us
    pallas_call x1, Pallas kernels, gather_weights(): call(functools.partial(gather_kernel, shape), outs, [IN_VMEM] * 2, (ANYWH...  94.1 us
    pallas_call x1, Pallas kernels, forward(): call(forward_kernel, outs, [IN_VMEM] * 3, (IN_VMEM,) * len(outs), scratch...  52.2 us
    pallas_call x1, Pallas kernels, attn_back(): call(attn_back_kernel, outs, ins, (IN_VMEM,) * 3, scratch, 'attn_back')  42.5 us
    pallas_call x1, Pallas kernels, feed_back(): call(feed_back_kernel, outs, ins, (IN_VMEM,) * 3, scratch, 'feed_back')  30.3 us
    unnamed x49, local copies, waits for them, and re-layouts  16 us
  transfers between devices with their start and end apart: 2, of which 0 were waited for; matrix products, arithmetic and copies ran while one was open for 1% of the time, Pallas kernels for 39%

profile of v1, /device:TPU:0, one launch (start us, length us, event | category | flops | bytes accessed | tf_op | source)
XLA Modules:
  0.0 432.7 jit_solution(2314536069989286627)
XLA Ops:
  1.3 1.3 convert_reduce_fusion
  2.6 0.8 bitcast_dynamic-update-slice_fusion.7
  3.4 0.8 bitcast_dynamic-update-slice_fusion.6
  4.3 0.8 bitcast_dynamic-update-slice_fusion.5
  5.1 0.8 bitcast_dynamic-update-slice_fusion.4
  6.0 0.8 bitcast_dynamic-update-slice_fusion.3
  6.8 0.8 bitcast_dynamic-update-slice_fusion.2
  7.7 0.8 bitcast_dynamic-update-slice_fusion.1
  8.5 0.8 bitcast_dynamic-update-slice_fusion.shards
  9.3 1.7 constant_dynamic-slice_fusion.3
  11.0 0.8 copy.42
  13.3 1.0 reshape.50.row_weight
  14.3 1.5 constant_dynamic-slice_fusion.2
  15.8 0.8 copy.43
  16.7 1.4 pad.15.clone
  18.1 1.4 pad.18.clone
  20.2 94.1 %gather_weights.1 = (bf16[8,2,4,2,2,64,512]{6,5,4,3,2,1,0:T(8,128)(2,1)}, f32[8,1024]{1,0:T(8,128)}) custom-call(bf16[8,64,512]{2,1,0:T(8,128)(2,1)} %copy-done.6, bf16[16,128]{1,0:T(8,128)(2,1)} %pad_select_fusion.tile), custom_call_target="tpu_custom_call" | custom-call | tf_op jit(solution)/shard_map/gather_weights/pallas_call | solution.py:700
  114.4 52.2 %forward.1 = (bf16[768,1024]{1,0:T(8,128)(2,1)}, bf16[768,1024]{1,0:T(8,128)(2,1)}, bf16[768,1024]{1,0:T(8,128)(2,1)}, bf16[768,1024]{1,0:T(8,128)(2,1)}, f32[6,...) custom-call(bf16[768,1024]{1,0:T(8,128)(2,1)} %bitcast.34, ...), custom_call_target="tpu_custom_call" | custom-call | tf_op jit(solution)/shard_map/forward/pallas_call | solution.py:724
  166.5 30.3 %feed_back.1 = (bf16[4,2,4,2,2,64,512]{6,5,4,3,2,1,0:T(8,128)(2,1)}, f32[768,1024]{1,0:T(8,128)}, f32[2,8,1024]{2,1,0:T(8,128)}) custom-call(bf16[768,1024]{1,0:T(8,128)(2,1)} %bitcast.36, f32[768,1]{1,0:T(8,128)} %reshape.50.row_weight, f32[8,1024]{1,0:T(8,128)} %get-tuple-element.38.vectors, bf16[8,2,4,2,2,64,512]{6,5,4,3,2,1,0:T(8,128)(2,1)} %get-tuple-element.39.g.g_all, ...), custom_call_target="tpu_custom_call" | custom-call | tf_op jit(solution)/shard_map/feed_back/pallas_call | solution.py:743
  196.8 42.5 %attn_back.1 = (bf16[4,2,4,2,2,64,512]{6,5,4,3,2,1,0:T(8,128)(2,1)}, f32[768,1024]{1,0:T(8,128)}, f32[2,8,1024]{2,1,0:T(8,128)}) custom-call(f32[768,1024]{1,0:T(8,128)} %get-tuple-element.45.gres, bf16[768,1024]{1,0:T(8,128)(2,1)} %bitcast.35, f32[8,1024]{1,0:T(8,128)} %get-tuple-element.38.vectors, ...), custom_call_target="tpu_custom_call" | custom-call | tf_op jit(solution)/shard_map/attn_back/pallas_call | solution.py:768
  239.3 0.7 broadcast_in_dim.7
  240.0 1.1 copy-done.3
  241.2 3.5 constant_dynamic-update-slice_fusion.1
  245.5 1.7 copy-done.5
  247.2 2.1 constant_dynamic-update-slice_fusion.3
  249.3 1.6 copy-done.4
  251.4 170.4 %scatter_grads.1 = (f32[64,512]{1,0:T(8,128)}, f32[64,512]{1,0:T(8,128)}, f32[64,512]{1,0:T(8,128)}, f32[64,512]{1,0:T(8,128)}, f32[64,1024]{1,0:T(8,128)}, /*index=5*/f32[64,1024]{1,0:T(8,128)}, f32[8,128]{1,0:T(8,128)}) custom-call(bf16[4,2,4,2,2,64,512]{6,5,4,3,2,1,0:T(8,128)(2,1)} %get-tuple-element.53.dw_a, ...), custom_call_target="tpu_custom_call" | custom-call | tf_op jit(solution)/shard_map/scatter_grads/pallas_call | solution.py:797
  421.8 0.7 constant_dynamic-slice_fusion
  423.0 1.2 constant_dynamic-update-slice_fusion.2
  424.3 3.9 constant_dynamic-update-slice_fusion
  430.9 0.7 copy.67
  431.6 0.7 copy.68
  (48 shorter events, 6.1 us)
Async XLA Ops:
  0.6 11.2 %copy-start = (s32[4,24]{1,0:T(4,128)S(1)}, s32[4,24]{1,0:T(4,128)}, u32[]{:S(2)}) copy-start(s32[4,24]{1,0:T(4,128)} %param.16) | copy-start | bytes 1156
  9.3 2.5 copy-start.6
  16.6 2.9 copy-start.13
  16.7 2.9 copy-start.14
  16.7 2.9 copy-start.15
  16.7 2.8 copy-start.16
  239.3 1.9 copy-start.3
  244.6 4.6 %copy-start.2 = (f32[4,24,15,1024]{3,1,2,0:T(8,128)}, f32[4,24,15,1024]{3,1,2,0:T(8,128)S(1)}, u32[]{:S(2)}) copy-start(f32[4,24,15,1024]{3,1,2,0:T(8,128)S(1)} %get-tuple-element.64) | copy-start | bytes 17694724
  244.6 2.5 copy-start.5
  244.6 179.6 %collective-permute-start.1 = (f32[2,24,15,1024]{3,1,2,0:T(8,128)}, f32[2,24,15,1024]{3,1,2,0:T(8,128)}, u32[]{:S(2)}, u32[]{:S(2)}) collective-permute-start(f32[2,24,15,1024]{3,1,2,0:T(8,128)} %get-tuple-element.65), channel_id=1, source_target_pairs={{0,1},{1,0},{2,3},{3,2},{4,5},{5,4},{6,7},{7,6},{8,9},{9,8},{10,11... | collective-permute-start | bytes 8847368 | tf_op jit(solution)/shard_map/ppermute | solution.py:875
  249.3 1.6 copy-start.4
  250.9 172.2 %collective-permute-start = (bf16[2,24,15,1024]{3,1,2,0:T(8,128)(2,1)}, bf16[2,24,15,1024]{3,1,2,0:T(8,128)(2,1)S(1)}, u32[]{:S(2)}, u32[]{:S(2)}) collective-permute-start(bf16[2,24,15,1024]{3,1,2,0:T(8,128)(2,1)} %get-tuple-element.67), channel_id=1, source_target_pairs={{0,1},{1,0},{2,3},{3,2},{4,5},{5,4},{6,7},{7,6},{8,9},{9,8},{10,11... | collective-permute-start | bytes 4423688 | tf_op jit(solution)/shard_map/ppermute | solution.py:875
  424.3 8.0 %copy-start.1 = (s32[4,24]{1,0:T(4,128)S(1)}, s32[4,24]{1,0:T(4,128)}, u32[]{:S(2)}) copy-start(s32[4,24]{1,0:T(4,128)} %param.16) | copy-start | bytes 1156
  424.3 4.0 copy-start.12
  424.3 4.6 %copy-start.11 = (f32[64,512]{1,0:T(8,128)S(1)}, f32[64,512]{1,0:T(8,128)}, u32[]{:S(2)}) copy-start(f32[64,512]{1,0:T(8,128)} %get-tuple-element.87) | copy-start | bytes 393220
  424.3 5.3 %copy-start.10 = (f32[64,512]{1,0:T(8,128)S(1)}, f32[64,512]{1,0:T(8,128)}, u32[]{:S(2)}) copy-start(f32[64,512]{1,0:T(8,128)} %get-tuple-element.88) | copy-start | bytes 393220
  424.3 5.9 %copy-start.9 = (f32[64,512]{1,0:T(8,128)S(1)}, f32[64,512]{1,0:T(8,128)}, u32[]{:S(2)}) copy-start(f32[64,512]{1,0:T(8,128)} %get-tuple-element.89) | copy-start | bytes 393220
  424.3 6.6 %copy-start.8 = (f32[64,1024]{1,0:T(8,128)S(1)}, f32[64,1024]{1,0:T(8,128)}, u32[]{:S(2)}) copy-start(f32[64,1024]{1,0:T(8,128)} %get-tuple-element.90) | copy-start | bytes 786436
  424.3 7.3 %copy-start.7 = (f32[64,1024]{1,0:T(8,128)S(1)}, f32[64,1024]{1,0:T(8,128)}, u32[]{:S(2)}) copy-start(f32[64,1024]{1,0:T(8,128)} %get-tuple-element.91) | copy-start | bytes 786436

commit v2 on v1

--- a/solution.py
+++ b/solution.py
@@ -21,6 +21,7 @@
 UPS = (U0, U1)
 DOWNS = (D0, D1)
 ORDERS = ("zxy", "zyx", "xyz", "zxy", "zyx", "xyz", "zxy", "zyx")
+BACK_ORDERS = ("xzy", "xyz", "zxy", "xzy", "yxz", "xzy", "yxz", "xzy")
 
 
 def nn(a, b):
@@ -561,7 +562,7 @@
 
 
 def attn_back_kernel(
-    gres, x, vectors, g_all, mix, probs, q, k, v, nrm, dw, gtok, vec, g, gal, galt, gm, gq, gk, gv, nrmt, gn, sems
+    gres, x, vectors, g_all, mix, probs, q, k, v, nrm, dw, gtok, gtok_low, vec, g, gal, galt, gm, gq, gk, gv, nrmt, gn, sems
 ):
     copies = fetch(g_all, g, sems, (O, Q, K, V))
     gain = vectors[0:1, :]
@@ -587,7 +588,9 @@
         pulled, normal = norm_pull(grad, x[rows, :].astype(F32), gain)
         vec[0] += fold_rows(grad * normal)
         vec[1] += fold_rows(grad)
-        gtok[rows, :] = gres[rows, :] + pulled
+        total = gres[rows, :] + pulled
+        gtok[rows, :] = total
+        gtok_low[rows, :] = total.astype(BF)
 
     row_loop(x.shape[0], last)
 
@@ -619,7 +622,7 @@
     segs = dw.shape[0]
     runs, start = {}, 0
     for seg in range(segs + 1):
-        order = ORDERS[seg][::-1] if seg < segs else "zx"
+        order = BACK_ORDERS[seg] if seg < segs else "zx"
         sems = (send.at[seg], recv.at[seg])
         if seg < segs:
             run = Scatter(place, dw.at[seg], "yzx", order, {}, hands.at[seg], sems)
@@ -748,7 +751,7 @@
 def attn_back(gres, x, vectors, g, mix, probs, q, k, v, nrm):
     rows, width = x.shape
     part = (4,) + g.shape[1:]
-    outs = (shape_of(part, BF), shape_of((rows, width), F32), shape_of((2, 8, width), F32))
+    outs = (shape_of(part, BF), shape_of((rows, width), F32), shape_of((rows, width), BF), shape_of((2, 8, width), F32))
     low = pltpu.VMEM((rows, width), BF)
     turned = pltpu.VMEM((width, rows), BF)
     scratch = [
@@ -765,7 +768,7 @@
     ]
     ins = [IN_VMEM] * 10
     ins[3] = ANYWHERE
-    return call(attn_back_kernel, outs, ins, (IN_VMEM,) * 3, scratch, "attn_back")(
+    return call(attn_back_kernel, outs, ins, (IN_VMEM,) * 4, scratch, "attn_back")(
         gres, x, vectors, g, mix, probs, q, k, v, nrm
     )
 
@@ -790,7 +793,7 @@
         dma((2,)),
     ]
     for seg in range(segs):
-        scratch += [pltpu.VMEM(s, BF) for s in inbox_shapes(count, "yzx", ORDERS[seg][::-1], (rows, cols))]
+        scratch += [pltpu.VMEM(s, BF) for s in inbox_shapes(count, "yzx", BACK_ORDERS[seg], (rows, cols))]
     scratch += [pltpu.VMEM(s, F32) for s in inbox_shapes({"z": nz, "x": nx}, "zx", "zx", (8, 128))]
     small, large = shape_of((rows, cols), F32), shape_of((rows, 2 * cols), F32)
     outs = (small, small, small, small, large, large, shape_of((8, 128), F32))
@@ -853,7 +856,7 @@
         vectors = jnp.pad(vectors, ((0, 4), (0, 0)))
     nrm, q, k, v, probs, mix, res, nrm2, active, slope, block_out = forward(x, vectors, g)
     dw_f, gres, vec_f = feed_back(cot, row_weight, vectors, g, active, slope, nrm2, res)
-    dw_a, gtok, vec_a = attn_back(gres, x, vectors, g, mix, probs, q, k, v, nrm)
+    dw_a, gtok, gtok_low, vec_a = attn_back(gres, x, vectors, g, mix, probs, q, k, v, nrm)
     if linked:
         grads = scatter_grads(shape, dw_a, dw_f, vec_a, vec_f)
         grads, vec = list(grads[:6]), grads[6]
@@ -866,19 +869,19 @@
         vec = jnp.concatenate((jnp.sum(vec_a, axis=1), jnp.sum(vec_f, axis=1)))
         vec = lax.psum_scatter(lax.psum(vec, "mp"), "dp", scatter_dimension=1, tiled=True)
 
-    def both_halves(array):
+    def both_halves(array, low):
         own = array.reshape(micro, series, PAD, width)[:, :, :patches]
         whole = jnp.zeros((micro * n_mp,) + own.shape[1:], own.dtype)
         whole = lax.dynamic_update_slice_in_dim(whole, own, y * micro, 0)
-        piece, at = own, y
+        piece, at = low.reshape(micro, series, PAD, width)[:, :, :patches], y
         for _ in range(n_mp - 1):
             piece = lax.ppermute(piece, "mp", [(i, (i + 1) % n_mp) for i in range(n_mp)])
             at = lax.rem(at + n_mp - 1, n_mp)
-            whole = lax.dynamic_update_slice_in_dim(whole, piece, at * micro, 0)
+            whole = lax.dynamic_update_slice_in_dim(whole, piece.astype(own.dtype), at * micro, 0)
         return whole
 
-    out = both_halves(block_out)
-    grad_tokens = both_halves(gtok)
+    out = both_halves(block_out, block_out)
+    grad_tokens = both_halves(gtok, gtok_low)
     return (out, grad_tokens, *grads, vec[0], vec[1], vec[2], vec[3])
 
 

time: 441 us -> 411 us (0.932)
  Pallas kernels: 389 us -> 362 us
    pallas_call x1, Pallas kernels: 170 us -> 143 us  [scatter_grads(): call(functools.partial(scatter_kernel, shape, None), outs, [ANYWHERE, ANY...]
    unnamed x49 -> x48, local copies, waits for them, and re-layouts: 16 us -> 16.8 us
  transfers between devices with their start and end apart: 2 -> 2, of which waited for: 0 -> 0; matrix products, arithmetic and copies ran while one was open for 1% -> 3% of each run, Pallas kernels for 39% -> 35%
where the time goes in v2:
time: 411 us; the launch traced here: 406 us
  Pallas kernels  362 us (88%)
  local copies, waits for them, and re-layouts  34.4 us (8%)
  other arithmetic  4.55 us (1%)
    pallas_call x1, Pallas kernels, scatter_grads(): call(functools.partial(scatter_kernel, shape, None), outs, [ANYWHERE, ANY...  143 us
    pallas_call x1, Pallas kernels, gather_weights(): call(functools.partial(gather_kernel, shape), outs, [IN_VMEM] * 2, (ANYWH...  94.1 us
    pallas_call x1, Pallas kernels, forward(): call(forward_kernel, outs, [IN_VMEM] * 3, (IN_VMEM,) * len(outs), scratch...  52.2 us
    pallas_call x1, Pallas kernels, attn_back(): call(attn_back_kernel, outs, ins, (IN_VMEM,) * 4, scratch, 'attn_back')  42.7 us
    pallas_call x1, Pallas kernels, feed_back(): call(feed_back_kernel, outs, ins, (IN_VMEM,) * 3, scratch, 'feed_back')  30.3 us
    unnamed x48, local copies, waits for them, and re-layouts  16.8 us
  transfers between devices with their start and end apart: 2, of which 0 were waited for; matrix products, arithmetic and copies ran while one was open for 3% of the time, Pallas kernels for 35%

profile of v2, /device:TPU:0, one launch (start us, length us, event | category | flops | bytes accessed | tf_op | source)
XLA Modules:
  0.0 405.8 jit_solution(199925714862948121)
XLA Ops:
  1.3 1.3 convert_reduce_fusion
  2.6 0.8 bitcast_dynamic-update-slice_fusion.7
  3.4 0.8 bitcast_dynamic-update-slice_fusion.6
  4.3 0.8 bitcast_dynamic-update-slice_fusion.5
  5.1 0.8 bitcast_dynamic-update-slice_fusion.4
  6.0 0.8 bitcast_dynamic-update-slice_fusion.3
  6.8 0.8 bitcast_dynamic-update-slice_fusion.2
  7.7 0.8 bitcast_dynamic-update-slice_fusion.1
  8.5 0.8 bitcast_dynamic-update-slice_fusion.shards
  9.3 1.7 constant_dynamic-slice_fusion.3
  11.0 0.8 copy.46
  13.3 1.0 reshape.55.row_weight
  14.3 1.5 constant_dynamic-slice_fusion.2
  15.8 0.8 copy.47
  16.7 1.4 pad.15.clone
  18.1 1.4 pad.18.clone
  20.2 94.1 %gather_weights.1 = (bf16[8,2,4,2,2,64,512]{6,5,4,3,2,1,0:T(8,128)(2,1)}, f32[8,1024]{1,0:T(8,128)}) custom-call(bf16[8,64,512]{2,1,0:T(8,128)(2,1)} %copy-done.5, bf16[16,128]{1,0:T(8,128)(2,1)} %pad_select_fusion.tile), custom_call_target="tpu_custom_call" | custom-call | tf_op jit(solution)/shard_map/gather_weights/pallas_call | solution.py:703
  114.3 52.2 %forward.1 = (bf16[768,1024]{1,0:T(8,128)(2,1)}, bf16[768,1024]{1,0:T(8,128)(2,1)}, bf16[768,1024]{1,0:T(8,128)(2,1)}, bf16[768,1024]{1,0:T(8,128)(2,1)}, f32[6,...) custom-call(bf16[768,1024]{1,0:T(8,128)(2,1)} %bitcast.36, ...), custom_call_target="tpu_custom_call" | custom-call | tf_op jit(solution)/shard_map/forward/pallas_call | solution.py:727
  166.5 30.3 %feed_back.1 = (bf16[4,2,4,2,2,64,512]{6,5,4,3,2,1,0:T(8,128)(2,1)}, f32[768,1024]{1,0:T(8,128)}, f32[2,8,1024]{2,1,0:T(8,128)}) custom-call(bf16[768,1024]{1,0:T(8,128)(2,1)} %bitcast.38, f32[768,1]{1,0:T(8,128)} %reshape.55.row_weight, f32[8,1024]{1,0:T(8,128)} %get-tuple-element.39.vectors, bf16[8,2,4,2,2,64,512]{6,5,4,3,2,1,0:T(8,128)(2,1)} %get-tuple-element.40.g.g_all, ...), custom_call_target="tpu_custom_call" | custom-call | tf_op jit(solution)/shard_map/feed_back/pallas_call | solution.py:746
  196.8 42.7 %attn_back.1 = (bf16[4,2,4,2,2,64,512]{6,5,4,3,2,1,0:T(8,128)(2,1)}, f32[768,1024]{1,0:T(8,128)}, bf16[768,1024]{1,0:T(8,128)(2,1)}, f32[2,8,1024]{2,1,0:T(8,128)}) custom-call(f32[768,1024]{1,0:T(8,128)} %get-tuple-element.46.gres, bf16[768,1024]{1,0:T(8,128)(2,1)} %bitcast.37, f32[8,1024]{1,0:T(8,128)} %get-tuple-element.39.vectors, ...), custom_call_target="tpu_custom_call" | custom-call | tf_op jit(solution)/shard_map/attn_back/pallas_call | solution.py:771
  239.5 3.5 copy.45
  243.5 2.0 broadcast_in_dim.6
  245.5 2.5 constant_dynamic-update-slice_fusion.1
  248.0 1.5 collective-permute-start
  249.5 142.9 %scatter_grads.1 = (f32[64,512]{1,0:T(8,128)}, f32[64,512]{1,0:T(8,128)}, f32[64,512]{1,0:T(8,128)}, f32[64,512]{1,0:T(8,128)}, f32[64,1024]{1,0:T(8,128)}, /*index=5*/f32[64,1024]{1,0:T(8,128)}, f32[8,128]{1,0:T(8,128)}) custom-call(bf16[4,2,4,2,2,64,512]{6,5,4,3,2,1,0:T(8,128)(2,1)} %get-tuple-element.55.dw_a, ...), custom_call_target="tpu_custom_call" | custom-call | tf_op jit(solution)/shard_map/scatter_grads/pallas_call | solution.py:800
  392.4 0.7 constant_dynamic-slice_fusion
  393.7 0.7 broadcast_in_dim.7
  394.5 1.1 copy-done.3
  395.6 2.0 copy_dynamic-update-slice_fusion
  397.6 1.9 convert_dynamic-update-slice_fusion
  399.6 1.2 constant_dynamic-update-slice_fusion
  401.4 1.1 copy.68
  (47 shorter events, 6.0 us)
Async XLA Ops:
  0.6 11.2 %copy-start = (s32[4,24]{1,0:T(4,128)S(1)}, s32[4,24]{1,0:T(4,128)}, u32[]{:S(2)}) copy-start(s32[4,24]{1,0:T(4,128)} %param.16) | copy-start | bytes 1156
  9.3 2.5 copy-start.5
  16.6 2.9 copy-start.12
  16.6 2.9 copy-start.13
  16.6 2.9 copy-start.14
  16.7 2.9 copy-start.15
  239.5 6.0 %copy-start.4 = (bf16[768,1024]{1,0:T(8,128)(2,1)S(1)}, bf16[768,1024]{1,0:T(8,128)(2,1)}, u32[]{:S(2)}) copy-start(bf16[768,1024]{1,0:T(8,128)(2,1)} %get-tuple-element.41) | copy-start | bytes 4718596
  243.0 154.6 %collective-permute-start.1 = (bf16[2,24,15,1024]{3,1,2,0:T(8,128)(2,1)}, bf16[2,24,15,1024]{3,1,2,0:T(8,128)(2,1)}, u32[]{:S(2)}, u32[]{:S(2)}) collective-permute-start(bf16[2,24,15,1024]{3,1,2,0:T(8,128)(2,1)} %copy.45), channel_id=1, source_target_pairs={{0,1},{1,0},{2,3},{3,2},{4,5},{5,4},{6,7},{7,6},{8,9},{9,8},{10,11... | collective-permute-start | bytes 4423688 | tf_op jit(solution)/shard_map/ppermute | solution.py:878
  248.0 151.6 %collective-permute-start = (bf16[2,24,15,1024]{3,1,2,0:T(8,128)(2,1)}, bf16[2,24,15,1024]{3,1,2,0:T(8,128)(2,1)S(1)}, u32[]{:S(2)}, u32[]{:S(2)}) collective-permute-start(bf16[2,24,15,1024]{3,1,2,0:T(8,128)(2,1)} %get-tuple-element.67), channel_id=1, source_target_pairs={{0,1},{1,0},{2,3},{3,2},{4,5},{5,4},{6,7},{7,6},{8,9},{9,8},{10,11... | collective-permute-start | bytes 4423688 | tf_op jit(solution)/shard_map/ppermute | solution.py:878
  393.7 1.9 copy-start.3
  397.6 3.2 copy-start.11
  397.6 3.8 copy-start.10
  397.6 5.0 %copy-start.9 = (f32[64,512]{1,0:T(8,128)S(1)}, f32[64,512]{1,0:T(8,128)}, u32[]{:S(2)}) copy-start(f32[64,512]{1,0:T(8,128)} %get-tuple-element.88) | copy-start | bytes 393220
  397.6 7.7 %copy-start.1 = (s32[4,24]{1,0:T(4,128)S(1)}, s32[4,24]{1,0:T(4,128)}, u32[]{:S(2)}) copy-start(s32[4,24]{1,0:T(4,128)} %param.16) | copy-start | bytes 1156
  399.5 5.8 %copy-start.2 = (f32[4,24,15,1024]{3,1,2,0:T(8,128)}, f32[4,24,15,1024]{3,1,2,0:T(8,128)S(1)}, u32[]{:S(2)}) copy-start(f32[4,24,15,1024]{3,1,2,0:T(8,128)S(1)} %convert_dynamic-update-slice_fusion) | copy-start | bytes 17694724
  399.5 3.7 copy-start.8
  399.5 4.4 %copy-start.7 = (f32[64,1024]{1,0:T(8,128)S(1)}, f32[64,1024]{1,0:T(8,128)}, u32[]{:S(2)}) copy-start(f32[64,1024]{1,0:T(8,128)} %get-tuple-element.90) | copy-start | bytes 786436
  399.5 5.1 %copy-start.6 = (f32[64,1024]{1,0:T(8,128)S(1)}, f32[64,1024]{1,0:T(8,128)}, u32[]{:S(2)}) copy-start(f32[64,1024]{1,0:T(8,128)} %get-tuple-element.91) | copy-start | bytes 786436
